TPU v7x, 32 devices: a whole 2x2x4 slice. The times are simulated.
32 devices in a mesh: lb: 8 (over y, x, core), rb: 4 (over z).
Axes of the slice: x: 2, y: 2, z: 4, core: 2. Of those that a mesh axis runs over, the one named last changes fastest.
Arguments:
- wavefunction: bfloat16 [3072, 4, 3072], P('lb', None, 'rb'), may hold values from -6 to 6
- left_environment: bfloat16 [8, 1024, 3072], P(None, 'lb'), may hold values from -0.109375 to 0.109375
- operator_left: float32 [8, 8, 2, 2], replicated, may hold values from -1.5 to 1.5
- operator_right: float32 [8, 8, 2, 2], replicated, may hold values from -1.5 to 1.5
- right_environment: bfloat16 [8, 3072, 3072], P(None, 'rb', 'lb'), may hold values from -0.0546875 to 0.0546875
- row_sector: int32 [8], replicated, may hold values from 0 to 3, never falling along the last dimension, each value on 1 to 4 neighbouring positions
Outputs:
- applied_state: bfloat16 [1024, 4, 3072], P('lb', None, 'rb')
- density: float32 [1024, 1024], P('lb', 'rb')
Inputs may be any that keep to these rules, and one draw needn't show every extreme that they name: `row_sector`: entry t is the sector of output rows t * 128 to (t + 1) * 128 - 1. Entries never fall along t; each sector holds 1 to 4 tiles, and one holds exactly 4.
All inputs are finite; a program needn't handle non-finite values.
Results may differ from a plain program's by a relative error of at most 0.013.
Values may be sent and summed in bfloat16 or wider, within the bound.
No kernel may reach another device: no remote copies, remote signals or barrier semaphores. Data moves between devices by JAX's collectives and lax.ppermute only.
A program may use at most 128 MiB of HBM per device.

v0:
```python
import math
import jax
import jax.numpy as jnp
from jax import lax
from jax.sharding import PartitionSpec as P

BOND_WIDTH = 3072
SECTOR_TILES = 4


def shifted(value, axis, by):
    devices = lax.axis_size(axis)
    pairs = [(i, i + by) for i in range(devices) if 0 <= i + by < devices]
    return lax.ppermute(value, axis, pairs)


def combine_operators(operator_left, operator_right):
    channels = operator_left.shape[0]
    joined = jnp.einsum(
        "aups,uvqt->avpqst", operator_left, operator_right, precision=lax.Precision.HIGHEST
    )
    return joined.reshape(channels, channels, 4, 4)


def label_at(labels, position):
    matches = jnp.arange(labels.shape[0], dtype=jnp.int32) == position
    return (jnp.sum(jnp.where(matches, labels, 0)), jnp.any(matches))


def tile_gram(left_tile, right_tile):
    return lax.dot_general(
        left_tile, right_tile, (((1,), (1,)), ((), ())), preferred_element_type=jnp.float32
    )


def fetch_tile(own_tile, offset):
    return shifted(own_tile, "lb", -offset)


def shards(
    wavefunction, left_environment, operator_left, operator_right, right_environment, row_sector
):
    channels, row_count, full_bond = left_environment.shape
    local_right = wavefunction.shape[2]
    left_matrix = left_environment.reshape(channels * row_count, full_bond)
    rows_piece = lax.all_gather(wavefunction, "lb", axis=0, tiled=True)
    flat_piece = rows_piece.reshape(rows_piece.shape[0], 4 * local_right)
    left_part = jnp.dot(left_matrix, flat_piece, preferred_element_type=jnp.float32)
    left_part = left_part.reshape(channels, row_count, 4, local_right)
    combined = combine_operators(operator_left, operator_right)
    mixed_part = jnp.einsum(
        "avyx,alxr->lyvr", combined, left_part, precision=lax.Precision.HIGHEST
    ).astype(jnp.bfloat16)
    mixed_matrix = mixed_part.reshape(row_count * 4, channels * local_right)
    columns_piece = lax.all_gather(right_environment, "lb", axis=2, tiled=True)
    flat_piece = columns_piece.reshape(channels * local_right, columns_piece.shape[2])
    partial_value = jnp.dot(mixed_matrix, flat_piece, preferred_element_type=jnp.float32)
    summed = lax.psum_scatter(
        partial_value.astype(jnp.bfloat16), "rb", scatter_dimension=1, tiled=True
    ).astype(jnp.float32)
    applied = summed.astype(jnp.bfloat16).reshape(row_count, 4, summed.shape[1])
    own_tile = applied.reshape(row_count, 4 * summed.shape[1])
    own_index = lax.axis_index("lb")
    tile_count = lax.axis_size("lb")
    reach_tiles = SECTOR_TILES - 1
    own_label = label_at(row_sector, own_index)[0]
    buffer = jnp.zeros((row_count, (tile_count + 2 * reach_tiles) * row_count), jnp.float32)

    def place_block(buffer, gram_block, offset):
        mate_index = own_index + offset
        mate_label, inside = label_at(row_sector, mate_index)
        keep_block = jnp.logical_and(inside, mate_label == own_label)
        gram_block = jnp.where(keep_block, gram_block, jnp.float32(0.0))
        column_start = (mate_index + reach_tiles) * row_count
        return lax.dynamic_update_slice(buffer, gram_block, (jnp.int32(0), column_start))

    buffer = place_block(buffer, tile_gram(own_tile, own_tile), 0)
    for distance in range(1, SECTOR_TILES):
        gram_block = tile_gram(own_tile, fetch_tile(own_tile, distance))
        buffer = place_block(buffer, gram_block, distance)
        returned = shifted(gram_block.astype(jnp.bfloat16), "lb", distance).astype(gram_block.dtype)
        buffer = place_block(buffer, returned.T, -distance)
    full_rows = buffer[:, reach_tiles * row_count : (reach_tiles + tile_count) * row_count]
    density = lax.psum_scatter(
        full_rows.astype(jnp.bfloat16), "rb", scatter_dimension=1, tiled=True
    ).astype(jnp.float32) * (1.0 / math.sqrt(4.0 * BOND_WIDTH))
    return (applied, density)


def solution(mesh):
    placed = (P("lb", None, "rb"), P(None, "lb", None), P(), P(), P(None, "rb", "lb"), P())
    return jax.shard_map(
        shards,
        mesh=mesh,
        in_specs=placed,
        out_specs=(P("lb", None, "rb"), P("lb", "rb")),
        check_vma=False,
    )
```

profile of v0, /device:TPU:0, one launch (start us, length us, event | category | flops | bytes accessed | tf_op | source)
XLA Modules:
  0.0 471.0 jit_solution(350183610917870450)
XLA Ops:
  9.2 0.7 copy.24
  9.9 101.4 %all-gather.3.cloned.1.call-done = bf16[3072,4,768]{2,1,0:T(4,128)(2,1)} async-done(((bf16[384,4,768]{2,1,0:T(4,128)(2,1)}), bf16[3072,4,768]{2,1,0:T(4,128)(2,1)}) %all-gather.3.cloned.1.call-update) | async-done | bytes 18874384 | tf_op jit(solution)/shard_map/all_gather | solution.py:46
  111.2 29.9 %copy.37 = bf16[3072,4,768]{0,2,1:T(8,128)(2,1)} copy(bf16[3072,4,768]{2,1,0:T(4,128)(2,1)} %all-gather.3.cloned.1.call-done) | data formatting | bytes 37748736 | tf_op jit(solution)/shard_map/reshape | solution.py:47
  141.2 27.1 %fusion = f32[8,128,4,768]{3,0,2,1:T(8,128)S(1)} fusion(bf16[3072,4,768]{0,2,1:T(8,128)(2,1)} %copy.37, bf16[8,128,3072,1]{2,1,0,3:T(8,128)(2,1)} %bitcast.55), kind=kOutput, calls=%fused_computation | convolution fusion | flops 19327352832 | bytes 37748736 | tf_op jit(solution)/shard_map/dot_general | solution.py:48
  168.3 11.4 %bitcast_convert_fusion = bf16[128,768,8,4]{1,2,3,0:T(8,128)(2,1)S(1)} fusion(f32[8,8,4,4,1]{1,0,3,2,4:T(8,128)S(1)} %bitcast.52, f32[8,128,4,768]{3,0,2,1:T(8,128)S(1)} %fusion), kind=kOutput, calls=%fused_computation.4 | convolution fusion | flops 1211105280 | bytes 18878464 | tf_op jit(solution)/shard_map/avyx,alxr->lyvr/dot_general | solution.py:51
  179.7 4.6 copy.43
  184.3 115.8 %all-gather.5.cloned.1.call-done = bf16[8,768,3072]{2,1,0:T(8,128)(2,1)} async-done(((bf16[8,768,384]{2,1,0:T(8,128)(2,1)}), bf16[8,768,3072]{2,1,0:T(8,128)(2,1)}) %all-gather.5.cloned.1.call-update) | async-done | bytes 37748752 | tf_op jit(solution)/shard_map/all_gather | solution.py:55
  300.1 27.4 %convolution_convert_fusion = bf16[512,3072]{1,0:T(8,128)(2,1)} fusion(bf16[512,6144]{1,0:T(8,128)(2,1)} %bitcast.51, bf16[6144,3072]{1,0:T(8,128)(2,1)} %bitcast.54), kind=kOutput, calls=%fused_computation.6 | convolution fusion | flops 19328925696 | bytes 47185920 | tf_op jit(solution)/shard_map/dot_general | solution.py:57
  327.7 60.5 %reduce-scatter.3.cloned.1.call-done = bf16[512,768]{1,0:T(8,128)(2,1)} async-done(((bf16[512,3072]{1,0:T(8,128)(2,1)}), bf16[512,768]{1,0:T(8,128)(2,1)}) %reduce-scatter.3.cloned.1.call-update) | async-done | bytes 786448 | tf_op jit(solution)/shard_map/reduce_scatter | solution.py:58
  388.2 1.6 reshape_reshape.3
  389.8 1.3 collective-permute-start
  392.4 0.8 fusion.16
  395.1 1.3 collective-permute-start.2
  396.4 1.0 fusion.7
  397.9 9.8 %collective-permute-start.1 = (bf16[128,128]{1,0:T(8,128)(2,1)S(1)}, bf16[128,128]{1,0:T(8,128)(2,1)S(1)}, u32[]{:S(2)}, u32[]{:S(2)}) collective-permute-start(bf16[128,128]{1,0:T(8,128)(2,1)S(1)} %get-tuple-element.10), channel_id=1, source_target_pairs={{0,4},{4,8},{8,12},{12,16},{16,20},{20,24},{24,28},{1,5},{5,9},{9,... | collective-permute-start | bytes 98312 | tf_op jit(solution)/shard_map/ppermute | solution.py:14
  412.8 1.3 collective-permute-start.4
  414.2 8.3 %collective-permute-done.2 = bf16[128,3072]{1,0:T(8,128)(2,1)} collective-permute-done((bf16[128,3072]{1,0:T(8,128)(2,1)S(1)}, bf16[128,3072]{1,0:T(8,128)(2,1)}, u32[]{:S(2)}, u32[]{:S(2)}) %collective-permute-start.2) | collective-permute-done | bytes 786464 | tf_op jit(solution)/shard_map/ppermute | solution.py:14
  422.5 1.5 select_dynamic-update-slice_fusion.1
  424.1 3.4 collective-permute-start.3
  433.2 7.3 %collective-permute-start.5 = (bf16[128,128]{1,0:T(8,128)(2,1)S(1)}, bf16[128,128]{1,0:T(8,128)(2,1)S(1)}, u32[]{:S(2)}, u32[]{:S(2)}) collective-permute-start(bf16[128,128]{1,0:T(8,128)(2,1)S(1)} %get-tuple-element.14), channel_id=1, source_target_pairs={{0,12},{4,16},{8,20},{12,24},{16,28},{1,13},{5,17},{9,21},{13,25},... | collective-permute-start | bytes 98312 | tf_op jit(solution)/shard_map/ppermute | solution.py:14
  443.2 0.7 slice.7
  444.0 1.1 reshape.28
  445.1 17.8 %reduce-scatter.5.cloned.1.call-done = bf16[128,256]{1,0:T(8,128)(2,1)} async-done(((bf16[128,1024]{1,0:T(8,128)(2,1)}), bf16[128,256]{1,0:T(8,128)(2,1)}) %reduce-scatter.5.cloned.1.call-update) | async-done | bytes 65552 | tf_op jit(solution)/shard_map/reduce_scatter | solution.py:84
  462.9 1.5 convert_multiply_fusion
  (45 shorter events, 7.7 us)
Async XLA Ops:
  7.2 1.6 copy-start
  7.2 1.6 copy-start.4
  7.2 104.0 %all-gather.3.cloned.1.call-start = ((), (), s32[]{:S(2)}) async-start(), calls=%async_computation.2 | async-start | bytes 21233664 | tf_op jit(solution)/shard_map/all_gather | solution.py:46
  7.9 292.2 %all-gather.5.cloned.1.call-start = ((), (), s32[]{:S(2)}) async-start(), calls=%async_computation.3 | async-start | bytes 42467328 | tf_op jit(solution)/shard_map/all_gather | solution.py:55
  8.7 379.5 %reduce-scatter.3.cloned.1.call-start = ((), (), s32[]{:S(2)}) async-start(), calls=%async_computation.4 | async-start | bytes 3932160 | tf_op jit(solution)/shard_map/reduce_scatter | solution.py:58
  141.2 27.1 %copy-start.3 = (f32[8,8,2,2,2,2]{1,0,5,4,3,2:T(8,128)S(1)}, f32[8,8,2,2,2,2]{1,0,5,4,3,2:T(8,128)}, u32[]{:S(2)}) copy-start(f32[8,8,2,2,2,2]{1,0,5,4,3,2:T(8,128)} %copy.24) | copy-start | bytes 12292
  300.1 92.3 %copy-start.5 = (s32[8]{0:T(128)S(1)}, s32[8]{0:T(128)}, u32[]{:S(2)}) copy-start(s32[8]{0:T(128)} %param.11) | copy-start | bytes 100
  327.6 136.8 %copy-start.1 = (f32[8,8,2,2]{1,3,2,0:T(2,128)S(1)}, f32[8,8,2,2]{1,3,2,0:T(2,128)}, u32[]{:S(2)}) copy-start(f32[8,8,2,2]{1,3,2,0:T(2,128)} %param.8) | copy-start | bytes 3076
  327.6 135.3 %reduce-scatter.5.cloned.1.call-start = ((), (), s32[]{:S(2)}) async-start(), calls=%async_computation.5 | async-start | bytes 327680 | tf_op jit(solution)/shard_map/reduce_scatter | solution.py:84
  388.2 55.9 %copy-start.2 = (bf16[512,768]{1,0:T(8,128)(2,1)S(1)}, bf16[512,768]{1,0:T(8,128)(2,1)}, u32[]{:S(2)}) copy-start(bf16[512,768]{1,0:T(8,128)(2,1)} %reduce-scatter.3.cloned.1.call-done) | copy-start | bytes 2359300
  389.8 7.7 %collective-permute-start = (bf16[128,3072]{1,0:T(8,128)(2,1)S(1)}, bf16[128,3072]{1,0:T(8,128)(2,1)S(1)}, u32[]{:S(2)}, u32[]{:S(2)}) collective-permute-start(bf16[128,3072]{1,0:T(8,128)(2,1)S(1)} %reshape_reshape.3), channel_id=1, source_target_pairs={{4,0},{8,4},{12,8},{16,12},{20,16},{24,20},{28,24},{5,1},{9,5},{13... | collective-permute-start | bytes 2359304 | tf_op jit(solution)/shard_map/ppermute | solution.py:14
  395.1 27.4 %collective-permute-start.2 = (bf16[128,3072]{1,0:T(8,128)(2,1)S(1)}, bf16[128,3072]{1,0:T(8,128)(2,1)}, u32[]{:S(2)}, u32[]{:S(2)}) collective-permute-start(bf16[128,3072]{1,0:T(8,128)(2,1)S(1)} %reshape_reshape.3), channel_id=1, source_target_pairs={{8,0},{12,4},{16,8},{20,12},{24,16},{28,20},{9,1},{13,5},{17,9},{2... | collective-permute-start | bytes 2359304 | tf_op jit(solution)/shard_map/ppermute | solution.py:14
  397.9 16.2 %collective-permute-start.1 = (bf16[128,128]{1,0:T(8,128)(2,1)S(1)}, bf16[128,128]{1,0:T(8,128)(2,1)S(1)}, u32[]{:S(2)}, u32[]{:S(2)}) collective-permute-start(bf16[128,128]{1,0:T(8,128)(2,1)S(1)} %get-tuple-element.10), channel_id=1, source_target_pairs={{0,4},{4,8},{8,12},{12,16},{16,20},{20,24},{24,28},{1,5},{5,9},{9,... | collective-permute-start | bytes 98312 | tf_op jit(solution)/shard_map/ppermute | solution.py:14
  412.8 20.0 %collective-permute-start.4 = (bf16[128,3072]{1,0:T(8,128)(2,1)S(1)}, bf16[128,3072]{1,0:T(8,128)(2,1)S(1)}, u32[]{:S(2)}, u32[]{:S(2)}) collective-permute-start(bf16[128,3072]{1,0:T(8,128)(2,1)S(1)} %reshape_reshape.3), channel_id=1, source_target_pairs={{12,0},{16,4},{20,8},{24,12},{28,16},{13,1},{17,5},{21,9},{25,13},... | collective-permute-start | bytes 2359304 | tf_op jit(solution)/shard_map/ppermute | solution.py:14
  424.1 8.6 %collective-permute-start.3 = (bf16[128,128]{1,0:T(8,128)(2,1)S(1)}, bf16[128,128]{1,0:T(8,128)(2,1)S(1)}, u32[]{:S(2)}, u32[]{:S(2)}) collective-permute-start(bf16[128,128]{1,0:T(8,128)(2,1)S(1)} %get-tuple-element.12), channel_id=1, source_target_pairs={{0,8},{4,12},{8,16},{12,20},{16,24},{20,28},{1,9},{5,13},{9,17},{1... | collective-permute-start | bytes 98312 | tf_op jit(solution)/shard_map/ppermute | solution.py:14
  433.2 9.9 %collective-permute-start.5 = (bf16[128,128]{1,0:T(8,128)(2,1)S(1)}, bf16[128,128]{1,0:T(8,128)(2,1)S(1)}, u32[]{:S(2)}, u32[]{:S(2)}) collective-permute-start(bf16[128,128]{1,0:T(8,128)(2,1)S(1)} %get-tuple-element.14), channel_id=1, source_target_pairs={{0,12},{4,16},{8,20},{12,24},{16,28},{1,13},{5,17},{9,21},{13,25},... | collective-permute-start | bytes 98312 | tf_op jit(solution)/shard_map/ppermute | solution.py:14
Sparse Core Ops, SparseCore 0:
  9.9 101.3 all-gather.2
  113.1 186.9 all-gather.4
  327.7 60.3 reduce-scatter.2
  444.1 18.7 reduce-scatter.4
where the time goes:
time: 472 us; the launch traced here: 471 us
  waiting for transfers between devices  305 us (65%)
  matrix products  69.7 us (15%)
  local copies, waits for them, and re-layouts  39.2 us (8%)
  between operations  25.5 us (5%)
  starting transfers between devices  24.6 us (5%)
  other arithmetic  6.78 us (1%)
    all_gather x1, waiting for transfers between devices, shards(): columns_piece = lax.all_gather(right_environment, 'lb', axis=2, tiled=True)  116 us
    all_gather x1, waiting for transfers between devices, shards(): rows_piece = lax.all_gather(wavefunction, 'lb', axis=0, tiled=True)  101 us
    reduce_scatter x1, waiting for transfers between devices, shards(): lax.psum_scatter(partial_value.astype(jnp.bfloat16), 'rb', scatter_dimens...  60.5 us
    reshape x1, local copies, waits for them, and re-layouts, shards(): flat_piece = rows_piece.reshape(rows_piece.shape[0], 4 * local_right)  29.9 us
    dot_general x1, matrix products, shards(): jnp.dot(mixed_matrix, flat_piece, preferred_element_type=jnp.float32)  27.4 us
    dot_general x1, matrix products, shards(): jnp.dot(left_matrix, flat_piece, preferred_element_type=jnp.float32)  27.1 us
    ppermute x6, starting transfers between devices, shifted(): return lax.ppermute(value, axis, pairs)  24.4 us
    reduce_scatter x1, waiting for transfers between devices, shards(): lax.psum_scatter(full_rows.astype(jnp.bfloat16), 'rb', scatter_dimension=...  17.8 us
  transfers between devices with their start and end apart: 10, of which 5 were waited for; matrix products, arithmetic and copies ran while one was open for 18% of the time, Pallas kernels for 0%

commit v1 on v0

--- a/solution.py
+++ b/solution.py
@@ -6,6 +6,12 @@
 
 BOND_WIDTH = 3072
 SECTOR_TILES = 4
+
+
+def in_order(blocks, dim):
+    blocks = jnp.moveaxis(blocks, 0, dim)
+    lengths = blocks.shape
+    return blocks.reshape(*lengths[:dim], lengths[dim] * lengths[dim + 1], *lengths[dim + 2 :])
 
 
 def shifted(value, axis, by):
@@ -43,7 +49,19 @@
     channels, row_count, full_bond = left_environment.shape
     local_right = wavefunction.shape[2]
     left_matrix = left_environment.reshape(channels * row_count, full_bond)
-    rows_piece = lax.all_gather(wavefunction, "lb", axis=0, tiled=True)
+    peers = lax.axis_size("lb")
+    pairs_2 = [(i_2, (i_2 + 1) % peers) for i_2 in range(peers)]
+    back = [(b, a) for a, b in pairs_2]
+    lower, upper = ([], [])
+    for step in range(peers - 1):
+        if step % 2 == 0:
+            lower.append(lax.ppermute(lower[-1] if lower else wavefunction, "lb", pairs_2))
+        else:
+            upper.append(lax.ppermute(upper[-1] if upper else wavefunction, "lb", back))
+    blocks = jnp.stack([*lower[::-1], wavefunction, *upper])
+    shift = lax.axis_index("lb") - len(lower)
+    blocks = blocks[(jnp.arange(peers) - shift) % peers]
+    rows_piece = in_order(blocks, 0)
     flat_piece = rows_piece.reshape(rows_piece.shape[0], 4 * local_right)
     left_part = jnp.dot(left_matrix, flat_piece, preferred_element_type=jnp.float32)
     left_part = left_part.reshape(channels, row_count, 4, local_right)

time: 472 us -> 676 us (1.43); the launches traced: 471 us -> 668 us
  waiting for transfers between devices: 305 us -> 403 us
  local copies, waits for them, and re-layouts: 39.2 us -> 106 us
  starting transfers between devices: 24.6 us -> 39.6 us
  other arithmetic: 6.78 us -> 20.1 us
    ppermute x0 -> x7, waiting for transfers between devices: none -> 314 us  [the longest x4 314 us: shards(): lax.ppermute(lower[-1] if lower else wavefunction, 'lb', pairs_2)]
    all_gather x1, waiting for transfers between devices: 116 us -> 0.01 us  [shards(): columns_piece = lax.all_gather(right_environment, 'lb', axis=2, tiled=True)]
    all_gather x1 -> x0, waiting for transfers between devices: 101 us -> none  [shards(): rows_piece = lax.all_gather(wavefunction, 'lb', axis=0, tiled=True)]
    unnamed x13 -> x24, local copies, waits for them, and re-layouts: 4.68 us -> 48 us
    gather x0 -> x3, local copies, waits for them, and re-layouts: none -> 39.1 us  [shards(): blocks = blocks[(jnp.arange(peers) - shift) % peers]]
    reshape x1, local copies, waits for them, and re-layouts: 29.9 us -> 12.8 us  [shards(): left_part = left_part.reshape(channels, row_count, 4, local_right)]
    ppermute x0 -> x7, starting transfers between devices: none -> 13.6 us  [the longest x4 13.5 us: shards(): lax.ppermute(lower[-1] if lower else wavefunction, 'lb', pairs_2)]
    unnamed x0 -> x1, other arithmetic: none -> 13.3 us
  transfers between devices with their start and end apart: 10 -> 16, of which waited for: 5 -> 7; matrix products, arithmetic and copies ran while one was open for 18% -> 25% of each run, Pallas kernels for 0% -> 0%
where the time goes in v1:
time: 676 us; the launch traced here: 668 us
  waiting for transfers between devices  403 us (60%)
  local copies, waits for them, and re-layouts  106 us (16%)
  matrix products  73.3 us (11%)
  starting transfers between devices  39.6 us (6%)
  between operations  25.6 us (4%)
  other arithmetic  20.1 us (3%)
    ppermute x4, waiting for transfers between devices, shards(): lax.ppermute(lower[-1] if lower else wavefunction, 'lb', pairs_2)  314 us
    reduce_scatter x1, waiting for transfers between devices, shards(): lax.psum_scatter(partial_value.astype(jnp.bfloat16), 'rb', scatter_dimens...  63.4 us
    unnamed x24, local copies, waits for them, and re-layouts  48 us
    gather x3, local copies, waits for them, and re-layouts, shards(): blocks = blocks[(jnp.arange(peers) - shift) % peers]  39.1 us
    dot_general x1, matrix products, shards(): jnp.dot(left_matrix, flat_piece, preferred_element_type=jnp.float32)  28.2 us
    dot_general x1, matrix products, shards(): jnp.dot(mixed_matrix, flat_piece, preferred_element_type=jnp.float32)  27.7 us
    ppermute x6, starting transfers between devices, shifted(): return lax.ppermute(value, axis, pairs)  25.9 us
    reduce_scatter x1, waiting for transfers between devices, shards(): lax.psum_scatter(full_rows.astype(jnp.bfloat16), 'rb', scatter_dimension=...  16.6 us
  transfers between devices with their start and end apart: 16, of which 7 were waited for; matrix products, arithmetic and copies ran while one was open for 25% of the time, Pallas kernels for 0%

profile of v1, /device:TPU:0, one launch (start us, length us, event | category | flops | bytes accessed | tf_op | source)
XLA Modules:
  0.0 667.7 jit_solution(899621160277763903)
XLA Ops:
  8.5 46.7 %collective-permute-done = bf16[384,4,768]{2,1,0:T(4,128)(2,1)S(1)} collective-permute-done((bf16[384,4,768]{2,1,0:T(4,128)(2,1)}, bf16[384,4,768]{2,1,0:T(4,128)(2,1)S(1)}, u32[]{:S(2)}, u32[]{:S(2)}) %collective-permute-start) | collective-permute-done | bytes 2359328 | tf_op jit(solution)/shard_map/ppermute | solution.py:58
  56.6 3.0 collective-permute-start.1
  59.6 92.9 %collective-permute-done.1 = bf16[384,4,768]{2,1,0:T(4,128)(2,1)S(1)} collective-permute-done((bf16[384,4,768]{2,1,0:T(4,128)(2,1)S(1)}, bf16[384,4,768]{2,1,0:T(4,128)(2,1)S(1)}, u32[]{:S(2)}, u32[]{:S(2)}) %collective-permute-start.1) | collective-permute-done | bytes 2359328 | tf_op jit(solution)/shard_map/ppermute | solution.py:58
  154.0 4.9 collective-permute-start.2
  158.9 98.6 %collective-permute-done.2 = bf16[384,4,768]{2,1,0:T(4,128)(2,1)} collective-permute-done((bf16[384,4,768]{2,1,0:T(4,128)(2,1)S(1)}, bf16[384,4,768]{2,1,0:T(4,128)(2,1)}, u32[]{:S(2)}, u32[]{:S(2)}) %collective-permute-start.2) | collective-permute-done | bytes 2359328 | tf_op jit(solution)/shard_map/ppermute | solution.py:58
  257.5 5.0 collective-permute-start.3
  263.9 75.9 %collective-permute-done.3 = bf16[384,4,768]{2,1,0:T(4,128)(2,1)} collective-permute-done((bf16[384,4,768]{2,1,0:T(4,128)(2,1)}, bf16[384,4,768]{2,1,0:T(4,128)(2,1)}, u32[]{:S(2)}, u32[]{:S(2)}) %collective-permute-start.3) | collective-permute-done | bytes 2359328 | tf_op jit(solution)/shard_map/ppermute | solution.py:58
  356.2 11.4 %fusion.12 = (bf16[8,384,4,384]{3,2,1,0:T(4,128)(2,1)}, bf16[8,384,4,384]{3,2,1,0:T(4,128)(2,1)}) fusion(bf16[8,384,4,768]{3,2,1,0:T(4,128)(2,1)S(1)} %bitcast_dynamic-update-slice_fusion), kind=kLoop, calls=%fused_computation.58 | loop fusion | bytes 37748736 | tf_op jit(solution)/shard_map/gather | solution.py:63
  367.6 13.9 %gather_fusion.1 = bf16[8,384,4,384]{3,2,1,0:T(4,128)(2,1)} fusion(bf16[8,384,4,384]{3,2,1,0:T(4,128)(2,1)} %get-tuple-element.10, s32[1024]{0:T(1024)S(1)} %pad_clamp_fusion), kind=kCustom, calls=%fused_computation.1 | custom fusion | bytes 18874400 | tf_op jit(solution)/shard_map/gather | solution.py:63
  381.4 13.8 %gather_fusion = bf16[8,384,4,384]{3,2,1,0:T(4,128)(2,1)} fusion(bf16[8,384,4,384]{3,2,1,0:T(4,128)(2,1)} %get-tuple-element.9, s32[1024]{0:T(1024)S(1)} %pad_clamp_fusion), kind=kCustom, calls=%fused_computation | custom fusion | bytes 18874400 | tf_op jit(solution)/shard_map/gather | solution.py:63
  395.3 13.3 %pad_maximum_fusion = bf16[8,384,4,768]{3,2,1,0:T(4,128)(2,1)} fusion(bf16[8,384,4,384]{3,2,1,0:T(4,128)(2,1)} %gather_fusion.1, bf16[8,384,4,384]{3,2,1,0:T(4,128)(2,1)} %gather_fusion), kind=kLoop, calls=%fused_computation.2 | loop fusion | flops 37748736 | bytes 37748736
  408.6 12.9 %copy.34 = bf16[384,8,4,768]{3,1,2,0:T(8,128)(2,1)S(1)} copy(bf16[384,8,4,768]{3,2,1,0:T(4,128)(2,1)} %bitcast.67) | data formatting | bytes 37748736
  421.5 28.2 %convolution_bitcast_fusion = f32[384,8,8,128]{3,1,2,0:T(8,128)} fusion(bf16[3072,3072]{1,0:T(8,128)(2,1)S(1)} %bitcast.70, bf16[1024,3072]{1,0:T(8,128)(2,1)} %bitcast.75), kind=kOutput, calls=%fused_computation.5 | convolution fusion | flops 19327352832 | bytes 37748736 | tf_op jit(solution)/shard_map/dot_general | solution.py:66
  449.8 12.2 %copy.35 = f32[384,8,8,128]{3,2,1,0:T(8,128)} copy(f32[384,8,8,128]{3,1,2,0:T(8,128)} %convolution_bitcast_fusion) | data formatting | bytes 25165824
  461.9 12.8 %copy.24 = f32[8,128,4,768,1]{3,0,2,4,1:T(8,128)} copy(f32[8,128,4,768,1]{1,0,3,2,4:T(8,128)} %bitcast.68) | data formatting | bytes 25165824 | tf_op jit(solution)/shard_map/reshape | solution.py:67
  474.8 14.1 %bitcast_convert_fusion = bf16[128,768,8,4]{1,2,3,0:T(8,128)(2,1)S(1)} fusion(f32[8,128,4,768,1]{3,0,2,4,1:T(8,128)} %copy.24, f32[8,8,4,4,1]{1,0,3,2,4:T(8,128)S(1)} %bitcast.72), kind=kOutput, calls=%fused_computation.3 | convolution fusion | flops 1211105280 | bytes 18878464 | tf_op jit(solution)/shard_map/avyx,alxr->lyvr/dot_general | solution.py:69
  488.8 4.6 copy.36
  493.5 27.7 %convolution_convert_fusion = bf16[512,3072]{1,0:T(8,128)(2,1)} fusion(bf16[512,6144]{1,0:T(8,128)(2,1)} %bitcast.71, bf16[6144,3072]{1,0:T(8,128)(2,1)} %bitcast.74), kind=kOutput, calls=%fused_computation.4 | convolution fusion | flops 19328925696 | bytes 47185920 | tf_op jit(solution)/shard_map/dot_general | solution.py:75
  521.2 63.4 %reduce-scatter.3.cloned.1.call-done = bf16[512,768]{1,0:T(8,128)(2,1)} async-done(((bf16[512,3072]{1,0:T(8,128)(2,1)}), bf16[512,768]{1,0:T(8,128)(2,1)}) %reduce-scatter.3.cloned.1.call-update) | async-done | bytes 786448 | tf_op jit(solution)/shard_map/reduce_scatter | solution.py:76
  594.3 9.9 %collective-permute-start.8 = (bf16[128,128]{1,0:T(8,128)(2,1)S(1)}, bf16[128,128]{1,0:T(8,128)(2,1)S(1)}, u32[]{:S(2)}, u32[]{:S(2)}) collective-permute-start(bf16[128,128]{1,0:T(8,128)(2,1)S(1)} %get-tuple-element.12), channel_id=1, source_target_pairs={{0,4},{4,8},{8,12},{12,16},{16,20},{20,24},{24,28},{1,5},{5,9},{9,... | collective-permute-start | bytes 98312 | tf_op jit(solution)/shard_map/ppermute | solution.py:20
  610.8 8.2 %collective-permute-done.9 = bf16[128,3072]{1,0:T(8,128)(2,1)S(1)} collective-permute-done((bf16[128,3072]{1,0:T(8,128)(2,1)S(1)}, bf16[128,3072]{1,0:T(8,128)(2,1)S(1)}, u32[]{:S(2)}, u32[]{:S(2)}) %collective-permute-start.9) | collective-permute-done | bytes 786464 | tf_op jit(solution)/shard_map/ppermute | solution.py:20
  619.3 3.5 collective-permute-start.10
  628.3 8.7 %collective-permute-start.12 = (bf16[128,128]{1,0:T(8,128)(2,1)S(1)}, bf16[128,128]{1,0:T(8,128)(2,1)S(1)}, u32[]{:S(2)}, u32[]{:S(2)}) collective-permute-start(bf16[128,128]{1,0:T(8,128)(2,1)S(1)} %get-tuple-element.16), channel_id=1, source_target_pairs={{0,12},{4,16},{8,20},{12,24},{16,28},{1,13},{5,17},{9,21},{13,25},... | collective-permute-start | bytes 98312 | tf_op jit(solution)/shard_map/ppermute | solution.py:20
  642.9 16.6 %reduce-scatter.5.cloned.1.call-done = bf16[128,256]{1,0:T(8,128)(2,1)} async-done(((bf16[128,1024]{1,0:T(8,128)(2,1)}), bf16[128,256]{1,0:T(8,128)(2,1)}) %reduce-scatter.5.cloned.1.call-update) | async-done | bytes 65552 | tf_op jit(solution)/shard_map/reduce_scatter | solution.py:102
  (74 shorter events, 39.9 us)
Async XLA Ops:
  7.2 255.4 %copy-start = (f32[8,8,2,2]{1,3,2,0:T(2,128)S(1)}, f32[8,8,2,2]{1,3,2,0:T(2,128)}, u32[]{:S(2)}) copy-start(f32[8,8,2,2]{1,3,2,0:T(2,128)} %param.8) | copy-start | bytes 3076
  7.2 341.5 %copy-start.2 = (bf16[384,4,768]{2,1,0:T(4,128)(2,1)S(1)}, bf16[384,4,768]{2,1,0:T(4,128)(2,1)}, u32[]{:S(2)}) copy-start(bf16[384,4,768]{2,1,0:T(4,128)(2,1)} %param.6) | copy-start | bytes 7077892
  7.2 486.3 %all-gather.2.cloned.1.call-start = ((), (), s32[]{:S(2)}) async-start(), calls=%async_computation.2 | async-start | bytes 42467328 | tf_op jit(solution)/shard_map/all_gather | solution.py:73
  7.9 576.7 %reduce-scatter.3.cloned.1.call-start = ((), (), s32[]{:S(2)}) async-start(), calls=%async_computation.3 | async-start | bytes 3932160 | tf_op jit(solution)/shard_map/reduce_scatter | solution.py:76
  8.0 47.2 %collective-permute-start = (bf16[384,4,768]{2,1,0:T(4,128)(2,1)}, bf16[384,4,768]{2,1,0:T(4,128)(2,1)S(1)}, u32[]{:S(2)}, u32[]{:S(2)}) collective-permute-start(bf16[384,4,768]{2,1,0:T(4,128)(2,1)} %param.6), channel_id=1, source_target_pairs={{0,4},{4,8},{8,12},{12,16},{16,20},{20,24},{24,28},{28,0},{1,5},{5... | collective-permute-start | bytes 7077896 | tf_op jit(solution)/shard_map/ppermute | solution.py:58
  55.2 1.4 copy-start.3
  56.6 95.9 %collective-permute-start.1 = (bf16[384,4,768]{2,1,0:T(4,128)(2,1)S(1)}, bf16[384,4,768]{2,1,0:T(4,128)(2,1)S(1)}, u32[]{:S(2)}, u32[]{:S(2)}) collective-permute-start(bf16[384,4,768]{2,1,0:T(4,128)(2,1)S(1)} %collective-permute-done), channel_id=1, source_target_pairs={{0,4},{4,8},{8,12},{12,16},{16,20},{20,24},{24,28},{28,0},{1,5},{5... | collective-permute-start | bytes 7077896 | tf_op jit(solution)/shard_map/ppermute | solution.py:58
  59.6 99.3 %collective-permute-start.4 = (bf16[384,4,768]{2,1,0:T(4,128)(2,1)}, bf16[384,4,768]{2,1,0:T(4,128)(2,1)}, u32[]{:S(2)}, u32[]{:S(2)}) collective-permute-start(bf16[384,4,768]{2,1,0:T(4,128)(2,1)} %param.6), channel_id=1, source_target_pairs={{4,0},{8,4},{12,8},{16,12},{20,16},{24,20},{28,24},{0,28},{5,1},{9... | collective-permute-start | bytes 7077896 | tf_op jit(solution)/shard_map/ppermute | solution.py:60
  152.5 1.5 copy-start.5
  154.0 103.5 %collective-permute-start.2 = (bf16[384,4,768]{2,1,0:T(4,128)(2,1)S(1)}, bf16[384,4,768]{2,1,0:T(4,128)(2,1)}, u32[]{:S(2)}, u32[]{:S(2)}) collective-permute-start(bf16[384,4,768]{2,1,0:T(4,128)(2,1)S(1)} %collective-permute-done.1), channel_id=1, source_target_pairs={{0,4},{4,8},{8,12},{12,16},{16,20},{20,24},{24,28},{28,0},{1,5},{5... | collective-permute-start | bytes 7077896 | tf_op jit(solution)/shard_map/ppermute | solution.py:58
  158.9 104.9 %collective-permute-start.5 = (bf16[384,4,768]{2,1,0:T(4,128)(2,1)}, bf16[384,4,768]{2,1,0:T(4,128)(2,1)}, u32[]{:S(2)}, u32[]{:S(2)}) collective-permute-start(bf16[384,4,768]{2,1,0:T(4,128)(2,1)} %collective-permute-done.4), channel_id=1, source_target_pairs={{4,0},{8,4},{12,8},{16,12},{20,16},{24,20},{28,24},{0,28},{5,1},{9... | collective-permute-start | bytes 7077896 | tf_op jit(solution)/shard_map/ppermute | solution.py:60
  257.5 82.2 %collective-permute-start.3 = (bf16[384,4,768]{2,1,0:T(4,128)(2,1)}, bf16[384,4,768]{2,1,0:T(4,128)(2,1)}, u32[]{:S(2)}, u32[]{:S(2)}) collective-permute-start(bf16[384,4,768]{2,1,0:T(4,128)(2,1)} %collective-permute-done.2), channel_id=1, source_target_pairs={{0,4},{4,8},{8,12},{12,16},{16,20},{20,24},{24,28},{28,0},{1,5},{5... | collective-permute-start | bytes 7077896 | tf_op jit(solution)/shard_map/ppermute | solution.py:58
  263.7 83.9 %copy-start.4 = (bf16[384,4,768]{2,1,0:T(4,128)(2,1)S(1)}, bf16[384,4,768]{2,1,0:T(4,128)(2,1)}, u32[]{:S(2)}) copy-start(bf16[384,4,768]{2,1,0:T(4,128)(2,1)} %copy-done.3) | copy-start | bytes 7077892
  263.8 91.3 %collective-permute-start.6 = (bf16[384,4,768]{2,1,0:T(4,128)(2,1)}, bf16[384,4,768]{2,1,0:T(4,128)(2,1)S(1)}, u32[]{:S(2)}, u32[]{:S(2)}) collective-permute-start(bf16[384,4,768]{2,1,0:T(4,128)(2,1)} %collective-permute-done.5), channel_id=1, source_target_pairs={{4,0},{8,4},{12,8},{16,12},{20,16},{24,20},{28,24},{0,28},{5,1},{9... | collective-permute-start | bytes 7077896 | tf_op jit(solution)/shard_map/ppermute | solution.py:60
  493.5 95.3 %copy-start.6 = (s32[8]{0:T(128)S(1)}, s32[8]{0:T(128)}, u32[]{:S(2)}) copy-start(s32[8]{0:T(128)} %param.11) | copy-start | bytes 100
  493.5 167.5 %copy-start.1 = (f32[8,8,2,2]{1,3,2,0:T(2,128)S(1)}, f32[8,8,2,2]{1,3,2,0:T(2,128)}, u32[]{:S(2)}) copy-start(f32[8,8,2,2]{1,3,2,0:T(2,128)} %param.8) | copy-start | bytes 3076
  521.2 138.3 %reduce-scatter.5.cloned.1.call-start = ((), (), s32[]{:S(2)}) async-start(), calls=%async_computation.4 | async-start | bytes 327680 | tf_op jit(solution)/shard_map/reduce_scatter | solution.py:102
  586.2 7.6 %collective-permute-start.7 = (bf16[128,3072]{1,0:T(8,128)(2,1)S(1)}, bf16[128,3072]{1,0:T(8,128)(2,1)S(1)}, u32[]{:S(2)}, u32[]{:S(2)}) collective-permute-start(bf16[128,3072]{1,0:T(8,128)(2,1)S(1)} %reshape_reshape.7), channel_id=1, source_target_pairs={{4,0},{8,4},{12,8},{16,12},{20,16},{24,20},{28,24},{5,1},{9,5},{13... | collective-permute-start | bytes 2359304 | tf_op jit(solution)/shard_map/ppermute | solution.py:20
  591.5 27.4 %collective-permute-start.9 = (bf16[128,3072]{1,0:T(8,128)(2,1)S(1)}, bf16[128,3072]{1,0:T(8,128)(2,1)S(1)}, u32[]{:S(2)}, u32[]{:S(2)}) collective-permute-start(bf16[128,3072]{1,0:T(8,128)(2,1)S(1)} %reshape_reshape.7), channel_id=1, source_target_pairs={{8,0},{12,4},{16,8},{20,12},{24,16},{28,20},{9,1},{13,5},{17,9},{2... | collective-permute-start | bytes 2359304 | tf_op jit(solution)/shard_map/ppermute | solution.py:20
  594.3 16.3 %collective-permute-start.8 = (bf16[128,128]{1,0:T(8,128)(2,1)S(1)}, bf16[128,128]{1,0:T(8,128)(2,1)S(1)}, u32[]{:S(2)}, u32[]{:S(2)}) collective-permute-start(bf16[128,128]{1,0:T(8,128)(2,1)S(1)} %get-tuple-element.12), channel_id=1, source_target_pairs={{0,4},{4,8},{8,12},{12,16},{16,20},{20,24},{24,28},{1,5},{5,9},{9,... | collective-permute-start | bytes 98312 | tf_op jit(solution)/shard_map/ppermute | solution.py:20
  609.3 18.6 %collective-permute-start.11 = (bf16[128,3072]{1,0:T(8,128)(2,1)S(1)}, bf16[128,3072]{1,0:T(8,128)(2,1)S(1)}, u32[]{:S(2)}, u32[]{:S(2)}) collective-permute-start(bf16[128,3072]{1,0:T(8,128)(2,1)S(1)} %reshape_reshape.7), channel_id=1, source_target_pairs={{12,0},{16,4},{20,8},{24,12},{28,16},{13,1},{17,5},{21,9},{25,13},... | collective-permute-start | bytes 2359304 | tf_op jit(solution)/shard_map/ppermute | solution.py:20
  619.3 8.4 %collective-permute-start.10 = (bf16[128,128]{1,0:T(8,128)(2,1)S(1)}, bf16[128,128]{1,0:T(8,128)(2,1)S(1)}, u32[]{:S(2)}, u32[]{:S(2)}) collective-permute-start(bf16[128,128]{1,0:T(8,128)(2,1)S(1)} %get-tuple-element.14), channel_id=1, source_target_pairs={{0,8},{4,12},{8,16},{12,20},{16,24},{20,28},{1,9},{5,13},{9,17},{1... | collective-permute-start | bytes 98312 | tf_op jit(solution)/shard_map/ppermute | solution.py:20
  628.3 11.2 %collective-permute-start.12 = (bf16[128,128]{1,0:T(8,128)(2,1)S(1)}, bf16[128,128]{1,0:T(8,128)(2,1)S(1)}, u32[]{:S(2)}, u32[]{:S(2)}) collective-permute-start(bf16[128,128]{1,0:T(8,128)(2,1)S(1)} %get-tuple-element.16), channel_id=1, source_target_pairs={{0,12},{4,16},{8,20},{12,24},{16,28},{1,13},{5,17},{9,21},{13,25},... | collective-permute-start | bytes 98312 | tf_op jit(solution)/shard_map/ppermute | solution.py:20
Sparse Core Ops, SparseCore 0:
  9.9 309.2 all-gather.1
  521.3 63.3 reduce-scatter.2
  640.6 18.7 reduce-scatter.4
